TPU v7x, 32 devices: a whole 2x2x4 slice. The times are simulated.
32 devices in a mesh: fsdp: 8 (over z, core), dp: 4 (over y, x).
Axes of the slice: x: 2, y: 2, z: 4, core: 2. Of those that a mesh axis runs over, the one named last changes fastest.
Arguments:
- embedded: bfloat16 [2, 1024, 32, 768], P(None, ('fsdp', 'dp')), may hold values from -6 to 6
- first_drop: int32 [2, 1024, 32, 768], P(None, ('fsdp', 'dp')), may hold values 0 or 1
- second_drop: int32 [2, 1024, 32, 768], P(None, ('fsdp', 'dp')), may hold values 0 or 1
- sent_lengths: int32 [1024], P(('fsdp', 'dp')), may hold values from 1 to 32, as said below
- out_cotangent: bfloat16 [2, 1024, 32, 768], P(None, ('fsdp', 'dp')), may hold values from -6 to 6
- triple_weight: bfloat16 [768, 2304], P(('fsdp', 'dp')), may hold values from -0.21875 to 0.21875
- query_value_bias: bfloat16 [1536], P(('fsdp', 'dp')), may hold values from -1.5 to 1.5
- mixer_weight: bfloat16 [768, 768], P(('fsdp', 'dp')), may hold values from -0.875 to 0.875
- mixer_bias: bfloat16 [768], P(('fsdp', 'dp')), may hold values from -1.5 to 1.5
- first_gain: bfloat16 [768], P(('fsdp', 'dp')), may hold values from 0.5 to 1.5
- first_shift: bfloat16 [768], P(('fsdp', 'dp')), may hold values from -1.5 to 1.5
- widen_weight: bfloat16 [768, 3072], P(('fsdp', 'dp')), may hold values from -0.21875 to 0.21875
- widen_bias: bfloat16 [3072], P(('fsdp', 'dp')), may hold values from -1.5 to 1.5
- narrow_weight: bfloat16 [3072, 768], P(('fsdp', 'dp')), may hold values from -0.109375 to 0.109375
- narrow_bias: bfloat16 [768], P(('fsdp', 'dp')), may hold values from -1.5 to 1.5
- second_gain: bfloat16 [768], P(('fsdp', 'dp')), may hold values from 0.5 to 1.5
- second_shift: bfloat16 [768], P(('fsdp', 'dp')), may hold values from -1.5 to 1.5
- pooler_weight: bfloat16 [768, 768], P(('fsdp', 'dp')), may hold values from -0.21875 to 0.21875
- pooler_bias: bfloat16 [768], P(('fsdp', 'dp')), may hold values from -1.5 to 1.5
Outputs:
- loss: float32 [], replicated
- outputs: bfloat16 [2, 1024, 32, 768], P(None, ('fsdp', 'dp'))
- input_grad: bfloat16 [2, 1024, 32, 768], P(None, ('fsdp', 'dp'))
- rms_stats: float32 [3], replicated
- grad_triple_weight: float32 [768, 2304], P(('fsdp', 'dp'))
- grad_query_value_bias: float32 [1536], P(('fsdp', 'dp'))
- grad_mixer_weight: float32 [768, 768], P(('fsdp', 'dp'))
- grad_mixer_bias: float32 [768], P(('fsdp', 'dp'))
- grad_first_gain: float32 [768], P(('fsdp', 'dp'))
- grad_first_shift: float32 [768], P(('fsdp', 'dp'))
- grad_widen_weight: float32 [768, 3072], P(('fsdp', 'dp'))
- grad_widen_bias: float32 [3072], P(('fsdp', 'dp'))
- grad_narrow_weight: float32 [3072, 768], P(('fsdp', 'dp'))
- grad_narrow_bias: float32 [768], P(('fsdp', 'dp'))
- grad_second_gain: float32 [768], P(('fsdp', 'dp'))
- grad_second_shift: float32 [768], P(('fsdp', 'dp'))
- grad_pooler_weight: float32 [768, 768], P(('fsdp', 'dp'))
- grad_pooler_bias: float32 [768], P(('fsdp', 'dp'))
Inputs may be any that keep to these rules, and one draw needn't show every extreme that they name: `sent_lengths`: the sentences of one device lie in a bucket of lengths b - 32 // 4 + 1 to b, where b lies between 8 and 32 ; the first sentence of each device has length b, and some device has b = 32.
All inputs are finite; a program needn't handle non-finite values. No bound on the sum of `first_drop` or of `second_drop` on one device may be relied on, other than what follows from the above.
Results may differ from a plain program's by a relative error of at most 0.014.
Values may be sent and summed in bfloat16 or wider, within the bound.
No kernel may reach another device: no remote copies, remote signals or barrier semaphores. Data moves between devices by JAX's collectives and lax.ppermute only.
A program may use at most 384 MiB of HBM per device.

v0:
```python
import jax
import jax.numpy as jnp
from jax import lax
from jax.sharding import PartitionSpec as P

HEADS = 12
DROP_SCALE = 1.0 / 0.9
SOFTMAX_TEMP = 0.05


def layer_norm(values, norm_gain, norm_shift):
    centred = values - jnp.mean(values, axis=-1, keepdims=True)
    spread = jnp.mean(centred * centred, axis=-1, keepdims=True)
    return centred * lax.rsqrt(spread + 1e-12) * norm_gain + norm_shift


def gelu_exact(values):
    return jax.nn.gelu(values, approximate=False)


def pool_unit(pooler_input):
    pooled = jnp.tanh(pooler_input)
    return pooled * lax.rsqrt(jnp.sum(pooled * pooled, axis=-1, keepdims=True) + 1e-06)


def rows_product(left_side, right_side):
    return lax.dot_general(
        left_side, right_side, (((0,), (0,)), ((), ())), preferred_element_type=jnp.float32
    )


def times_transpose(left_side, right_side):
    return lax.dot_general(
        left_side, right_side, (((1,), (1,)), ((), ())), preferred_element_type=jnp.float32
    )


def column_sums(values):
    return jnp.sum(values, axis=0, dtype=jnp.float32)


def on_device(
    embedded,
    first_drop,
    second_drop,
    sent_lengths,
    out_cotangent,
    triple_weight,
    query_value_bias,
    mixer_weight,
    mixer_bias,
    first_gain,
    first_shift,
    widen_weight,
    widen_bias,
    narrow_weight,
    narrow_bias,
    second_gain,
    second_shift,
    pooler_weight,
    pooler_bias,
):
    view_count, sent_count, length, model_width = embedded.shape
    head_count = HEADS
    head_width = model_width // head_count
    seq_count = view_count * sent_count
    row_count = seq_count * length
    scale_inner = head_width ** (-0.5)
    triple, query_value, mixer, mixer_shift, gain_one, shift_one = (
        lax.all_gather(triple_weight, ("fsdp", "dp"), axis=0, tiled=True),
        lax.all_gather(query_value_bias, ("fsdp", "dp"), axis=0, tiled=True),
        lax.all_gather(mixer_weight, ("fsdp", "dp"), axis=0, tiled=True),
        lax.all_gather(mixer_bias, ("fsdp", "dp"), axis=0, tiled=True),
        lax.all_gather(first_gain, ("fsdp", "dp"), axis=0, tiled=True),
        lax.all_gather(first_shift, ("fsdp", "dp"), axis=0, tiled=True),
    )
    valid_bool = lax.iota(jnp.int32, length)[None, :] < sent_lengths[:, None]
    valid_mask = valid_bool.astype(jnp.float32)
    valid_rows = jnp.broadcast_to(valid_mask[None], (view_count, sent_count, length)).reshape(
        row_count, 1
    )
    valid_keys = jnp.tile(valid_bool, (view_count, 1))
    row_data = embedded.reshape(row_count, model_width)
    drop_one = first_drop.reshape(row_count, model_width).astype(jnp.float32) * DROP_SCALE
    drop_two = second_drop.reshape(row_count, model_width).astype(jnp.float32) * DROP_SCALE
    query_value_f = query_value.astype(jnp.float32)
    bias_full = jnp.concatenate(
        [
            query_value_f[:model_width],
            jnp.zeros((model_width,), jnp.float32),
            query_value_f[model_width:],
        ]
    )
    packed = (jnp.dot(row_data, triple, preferred_element_type=jnp.float32) + bias_full).astype(
        jnp.bfloat16
    )
    packed = packed.reshape(seq_count, length, 3, head_count, head_width)
    queries = packed[:, :, 0]
    key_rows = packed[:, :, 1]
    values = packed[:, :, 2]
    scores = (
        jnp.einsum("sqhe,skhe->shqk", queries, key_rows, preferred_element_type=jnp.float32)
        * scale_inner
    )
    scores = jnp.where(valid_keys[:, None, None, :], scores, -1000000000.0)
    attention = jax.nn.softmax(scores, axis=-1)
    attention_low = attention.astype(jnp.bfloat16)
    context = jnp.einsum(
        "shqk,skhe->sqhe", attention_low, values, preferred_element_type=jnp.float32
    )
    context = context.reshape(row_count, model_width).astype(jnp.bfloat16)
    branch = jnp.dot(context, mixer, preferred_element_type=jnp.float32) + mixer_shift.astype(
        jnp.float32
    )
    attn_part = branch * drop_one
    input_rows = row_data.astype(jnp.float32)
    residual = input_rows + attn_part
    hidden, norm_one_back = jax.vjp(
        layer_norm, residual, gain_one.astype(jnp.float32), shift_one.astype(jnp.float32)
    )
    hidden_low = hidden.astype(jnp.bfloat16)
    widen, widen_shift, narrow, narrow_shift, gain_two, shift_two, pooler, pooler_shift = (
        lax.all_gather(widen_weight, ("fsdp", "dp"), axis=0, tiled=True),
        lax.all_gather(widen_bias, ("fsdp", "dp"), axis=0, tiled=True),
        lax.all_gather(narrow_weight, ("fsdp", "dp"), axis=0, tiled=True),
        lax.all_gather(narrow_bias, ("fsdp", "dp"), axis=0, tiled=True),
        lax.all_gather(second_gain, ("fsdp", "dp"), axis=0, tiled=True),
        lax.all_gather(second_shift, ("fsdp", "dp"), axis=0, tiled=True),
        lax.all_gather(pooler_weight, ("fsdp", "dp"), axis=0, tiled=True),
        lax.all_gather(pooler_bias, ("fsdp", "dp"), axis=0, tiled=True),
    )
    widened = jnp.dot(hidden_low, widen, preferred_element_type=jnp.float32) + widen_shift.astype(
        jnp.float32
    )
    active_f, gelu_back = jax.vjp(gelu_exact, widened)
    active = active_f.astype(jnp.bfloat16)
    narrowed = jnp.dot(active, narrow, preferred_element_type=jnp.float32) + narrow_shift.astype(
        jnp.float32
    )
    ffn_part = narrowed * drop_two
    second = hidden + ffn_part
    normed, norm_two_back = jax.vjp(
        layer_norm, second, gain_two.astype(jnp.float32), shift_two.astype(jnp.float32)
    )
    outputs = (normed * valid_rows).astype(jnp.bfloat16)
    first_token = outputs.reshape(view_count, sent_count, length, model_width)[:, :, 0].reshape(
        seq_count, model_width
    )
    pooler_input = jnp.dot(
        first_token, pooler, preferred_element_type=jnp.float32
    ) + pooler_shift.astype(jnp.float32)
    unit_f, pool_back = jax.vjp(pool_unit, pooler_input)
    unit_rows = unit_f.astype(jnp.bfloat16).reshape(view_count, sent_count, model_width)
    first_unit = unit_rows[0]
    second_unit = unit_rows[1]
    every_second = lax.all_gather(second_unit, ("fsdp", "dp"), axis=0, tiled=True)
    sentence_total = every_second.shape[0]
    cosine_similarity = times_transpose(first_unit, every_second)
    scaled_logits = cosine_similarity / SOFTMAX_TEMP
    log_total = jax.nn.logsumexp(scaled_logits, axis=-1)
    own_columns = lax.axis_index(("fsdp", "dp")) * sent_count + lax.iota(jnp.int32, sent_count)
    target_indicator = (
        lax.iota(jnp.int32, sentence_total)[None, :] == own_columns[:, None]
    ).astype(jnp.float32)
    positive = jnp.sum(target_indicator * scaled_logits, axis=-1)
    loss_part = jnp.sum(log_total - positive)
    square_sums = jnp.stack(
        [
            jnp.sum(valid_rows * input_rows * input_rows),
            jnp.sum(valid_rows * attn_part * attn_part),
            jnp.sum(valid_rows * ffn_part * ffn_part),
            2.0 * jnp.sum(sent_lengths).astype(jnp.float32),
        ]
    )
    loss_total, sums_total = lax.psum((loss_part, square_sums), ("fsdp", "dp"))
    loss_value = loss_total / sentence_total
    rms_stats = jnp.sqrt(sums_total[:3] / (sums_total[3] * model_width))
    softmax_probs = jnp.exp(scaled_logits - log_total[:, None])
    similarity_grad = ((softmax_probs - target_indicator) / SOFTMAX_TEMP).astype(jnp.bfloat16)
    dfirst = jnp.dot(similarity_grad, every_second, preferred_element_type=jnp.float32)
    dsecond_all = rows_product(similarity_grad, first_unit)
    dsecond_unit = lax.psum_scatter(dsecond_all, ("fsdp", "dp"), scatter_dimension=0, tiled=True)
    widen_back, narrow_back, pooler_back = (
        lax.all_gather(widen_weight, ("fsdp", "dp"), axis=0, tiled=True),
        lax.all_gather(narrow_weight, ("fsdp", "dp"), axis=0, tiled=True),
        lax.all_gather(pooler_weight, ("fsdp", "dp"), axis=0, tiled=True),
    )
    dunit = jnp.concatenate([dfirst, dsecond_unit], axis=0)
    dpooler = pool_back(dunit)[0].astype(jnp.bfloat16)
    grad_pooler_weight = rows_product(first_token, dpooler)
    grad_pooler_bias = column_sums(dpooler)
    dfirst_token = times_transpose(dpooler, pooler_back).reshape(
        view_count, sent_count, model_width
    )
    dnormed = out_cotangent.astype(jnp.float32)
    dnormed = dnormed.at[:, :, 0].add(dfirst_token).reshape(row_count, model_width) * valid_rows
    dsecond, grad_second_gain, grad_second_shift = norm_two_back(dnormed)
    dnarrow = (dsecond * drop_two).astype(jnp.bfloat16)
    grad_narrow_weight = rows_product(active, dnarrow)
    grad_narrow_bias = column_sums(dnarrow)
    dactive = times_transpose(dnarrow, narrow_back)
    dwidened = gelu_back(dactive)[0].astype(jnp.bfloat16)
    grad_widen_weight = rows_product(hidden_low, dwidened)
    grad_widen_bias = column_sums(dwidened)
    dhidden = dsecond + times_transpose(dwidened, widen_back)
    ffn_grads = (
        lax.psum_scatter(grad_widen_weight, ("fsdp", "dp"), scatter_dimension=0, tiled=True),
        lax.psum_scatter(grad_widen_bias, ("fsdp", "dp"), scatter_dimension=0, tiled=True),
        lax.psum_scatter(grad_narrow_weight, ("fsdp", "dp"), scatter_dimension=0, tiled=True),
        lax.psum_scatter(grad_narrow_bias, ("fsdp", "dp"), scatter_dimension=0, tiled=True),
        lax.psum_scatter(grad_second_gain, ("fsdp", "dp"), scatter_dimension=0, tiled=True),
        lax.psum_scatter(grad_second_shift, ("fsdp", "dp"), scatter_dimension=0, tiled=True),
        lax.psum_scatter(grad_pooler_weight, ("fsdp", "dp"), scatter_dimension=0, tiled=True),
        lax.psum_scatter(grad_pooler_bias, ("fsdp", "dp"), scatter_dimension=0, tiled=True),
    )
    triple_back, mixer_back = (
        lax.all_gather(triple_weight, ("fsdp", "dp"), axis=0, tiled=True),
        lax.all_gather(mixer_weight, ("fsdp", "dp"), axis=0, tiled=True),
    )
    dresidual, grad_first_gain, grad_first_shift = norm_one_back(dhidden)
    dbranch = (dresidual * drop_one).astype(jnp.bfloat16)
    grad_mixer_weight = rows_product(context, dbranch)
    grad_mixer_bias = column_sums(dbranch)
    dcontext = (
        times_transpose(dbranch, mixer_back)
        .astype(jnp.bfloat16)
        .reshape(seq_count, length, head_count, head_width)
    )
    dattention = jnp.einsum("sqhe,skhe->shqk", dcontext, values, preferred_element_type=jnp.float32)
    dvalues = jnp.einsum(
        "shqk,sqhe->skhe", attention_low, dcontext, preferred_element_type=jnp.float32
    )
    dscores = (
        attention * (dattention - jnp.sum(attention * dattention, axis=-1, keepdims=True))
    ).astype(jnp.bfloat16)
    dqueries = (
        jnp.einsum("shqk,skhe->sqhe", dscores, key_rows, preferred_element_type=jnp.float32)
        * scale_inner
    )
    dkey_rows = (
        jnp.einsum("shqk,sqhe->skhe", dscores, queries, preferred_element_type=jnp.float32)
        * scale_inner
    )
    dpacked = (
        jnp.stack([dqueries, dkey_rows, dvalues], axis=2)
        .astype(jnp.bfloat16)
        .reshape(row_count, 3 * model_width)
    )
    grad_triple_weight = rows_product(row_data, dpacked)
    packed_sums = column_sums(dpacked)
    grad_query_value_bias = jnp.concatenate(
        [packed_sums[:model_width], packed_sums[2 * model_width :]]
    )
    input_grad = (
        (dresidual + times_transpose(dpacked, triple_back))
        .astype(jnp.bfloat16)
        .reshape(embedded.shape)
    )
    attn_grads = (
        lax.psum_scatter(grad_triple_weight, ("fsdp", "dp"), scatter_dimension=0, tiled=True),
        lax.psum_scatter(grad_query_value_bias, ("fsdp", "dp"), scatter_dimension=0, tiled=True),
        lax.psum_scatter(grad_mixer_weight, ("fsdp", "dp"), scatter_dimension=0, tiled=True),
        lax.psum_scatter(grad_mixer_bias, ("fsdp", "dp"), scatter_dimension=0, tiled=True),
        lax.psum_scatter(grad_first_gain, ("fsdp", "dp"), scatter_dimension=0, tiled=True),
        lax.psum_scatter(grad_first_shift, ("fsdp", "dp"), scatter_dimension=0, tiled=True),
    )
    outputs = outputs.reshape(embedded.shape)
    return (
        loss_value,
        outputs,
        input_grad,
        rms_stats,
        attn_grads[0],
        attn_grads[1],
        attn_grads[2],
        attn_grads[3],
        attn_grads[4],
        attn_grads[5],
        ffn_grads[0],
        ffn_grads[1],
        ffn_grads[2],
        ffn_grads[3],
        ffn_grads[4],
        ffn_grads[5],
        ffn_grads[6],
        ffn_grads[7],
    )


def solution(mesh):
    in_specs = (
        P(None, ("fsdp", "dp"), None, None),
        P(None, ("fsdp", "dp"), None, None),
        P(None, ("fsdp", "dp"), None, None),
        P(("fsdp", "dp")),
        P(None, ("fsdp", "dp"), None, None),
        P(("fsdp", "dp"), None),
        P(("fsdp", "dp")),
        P(("fsdp", "dp"), None),
        P(("fsdp", "dp")),
        P(("fsdp", "dp")),
        P(("fsdp", "dp")),
        P(("fsdp", "dp"), None),
        P(("fsdp", "dp")),
        P(("fsdp", "dp"), None),
        P(("fsdp", "dp")),
        P(("fsdp", "dp")),
        P(("fsdp", "dp")),
        P(("fsdp", "dp"), None),
        P(("fsdp", "dp")),
    )
    out_specs = (
        P(),
        P(None, ("fsdp", "dp"), None, None),
        P(None, ("fsdp", "dp"), None, None),
        P(),
        P(("fsdp", "dp"), None),
        P(("fsdp", "dp")),
        P(("fsdp", "dp"), None),
        P(("fsdp", "dp")),
        P(("fsdp", "dp")),
        P(("fsdp", "dp")),
        P(("fsdp", "dp"), None),
        P(("fsdp", "dp")),
        P(("fsdp", "dp"), None),
        P(("fsdp", "dp")),
        P(("fsdp", "dp")),
        P(("fsdp", "dp")),
        P(("fsdp", "dp"), None),
        P(("fsdp", "dp")),
    )
    return jax.shard_map(
        on_device, mesh=mesh, in_specs=in_specs, out_specs=out_specs, check_vma=False
    )
```

profile of v0, /device:TPU:0, one launch (start us, length us, event | category | flops | bytes accessed | tf_op | source)
XLA Modules:
  0.0 1161.4 jit_solution(15726885025658911073)
XLA Ops:
  10.6 0.8 dynamic-update-slice.10
  16.5 0.8 dynamic-update-slice.7
  17.4 0.8 dynamic-update-slice.3
  18.2 42.6 %all-reduce.19 = (bf16[1536]{0:T(1024)(128)(2,1)S(1)}, bf16[768]{0:T(1024)(128)(2,1)S(1)}, bf16[768]{0:T(1024)(128)(2,1)S(1)}, bf16[768]{0:T(1024)(128)(2,1)S(1)...) all-reduce(bf16[1536]{0:T(1024)(128)(2,1)S(1)} %dynamic-update-slic, ...), channel_id=1, replica_groups=mesh['fsdp'=8,'dp'=4] {'fsdp','dp'}, use_global_device_ids=true, to_apply=%add | all-reduce | flops 9984 | bytes 39936
  61.5 6.7 convert_multiply_fusion.1
  68.8 7.0 convert_multiply_fusion
  78.3 11.8 %add_convert_fusion.1 = bf16[2048,2304]{1,0:T(8,128)(2,1)} fusion(bf16[2048,768]{1,0:T(8,128)(2,1)S(1)} %bitcast.108, bf16[768,2304]{1,0:T(8,128)(2,1)} %all-gather.7.cloned.1.call-done, f32[2304]{0:T(1024)S(1)} %pad_maximum_fusion.1), kind=kOutput, calls=%fused_computation.21 | convolution fusion | flops 7257194496 | bytes 16131072 | tf_op jit(solution)/shard_map/dot_general | solution.py:94
  90.1 28.7 %reshape.277 = bf16[64,32,3,12,64]{4,3,2,1,0:T(8,128)(2,1)} reshape(bf16[2048,2304]{1,0:T(8,128)(2,1)} %add_convert_fusion.1) | data formatting | bytes 18874368 | tf_op jit(solution)/shard_map/reshape | solution.py:97
  118.8 17.1 %fusion.57 = (bf16[64,32,1,12,64]{4,3,2,1,0:T(8,128)(2,1)}, bf16[64,32,1,12,64]{4,3,2,1,0:T(8,128)(2,1)}, bf16[64,32,1,12,64]{4,3,2,1,0:T(8,128)(2,1)}) fusion(bf16[64,32,3,12,64]{4,3,2,1,0:T(8,128)(2,1)} %reshape.277), kind=kLoop, calls=%fused_computation.134 | loop fusion | bytes 18874368 | tf_op jit(solution)/shard_map/slice | solution.py:99
  136.0 13.9 %fusion.22 = f32[64,12,32,32]{2,3,1,0:T(8,128)} fusion(bf16[64,32,1,12,64]{4,3,2,1,0:T(8,128)(2,1)} %get-tuple-element.136, bf16[64,32,1,12,64]{4,3,2,1,0:T(8,128)(2,1)} %get-tuple-element.135), kind=kOutput, calls=%fused_computation.75 | convolution fusion | flops 100663296 | bytes 9437184 | tf_op jit(solution)/shard_map/sqhe,skhe->shqk/dot_general | solution.py:102
  149.9 16.3 %fusion.60 = (f32[64,12,32]{2,1,0:T(8,128)S(1)}, f32[64,12,32,32]{2,3,1,0:T(8,128)}) fusion(f32[64,12,32,32]{2,3,1,0:T(8,128)} %fusion.22, pred[64,32]{1,0:T(8,128)(4,1)S(1)} %bitcast.115), kind=kOutput, calls=%fused_computation.137 | output fusion | flops 4718623 | bytes 6391808 | tf_op jit(solution)/shard_map/sub | solution.py:106
  166.1 11.4 convert_bitcast_fusion
  177.5 11.3 copy.62
  188.8 11.5 convert_element_type.145
  200.4 10.2 fusion.56
  210.6 2.6 copy-done.2
  213.2 0.8 multiply_reduce_fusion.7
  214.7 70.2 %multiply_convert_fusion = (bf16[2048,3072]{1,0:T(8,128)(2,1)}, f32[2048,3072]{1,0:T(8,128)}, f32[2048,3072]{1,0:T(8,128)}) fusion(f32[3072]{0:T(1024)S(1)} %convert_element_type.151, bf16[768,3072]{1,0:T(8,128)(2,1)} %all-gather.11.cloned.1.call-done, f32[2048,768]{1,0:T(8,128)} %copy-done.2, f32[768]{0:T(1024)S(1)} %convert_element_type.149, ...), kind=kOutput, calls=%fused_computation.7 | convolution fusion | flops 10086776832 | bytes 73959424 | tf_op jit(solution)/shard_map/dot_general | solution.py:132
  284.9 19.6 %fusion.53 = (f32[2048]{0:T(1024)S(1)}, f32[2048,768]{1,0:T(8,128)S(1)}, f32[2048,768]{1,0:T(8,128)}) fusion(f32[768]{0:T(1024)S(1)} %convert_element_type.149, f32[768]{0:T(1024)S(1)} %convert_element_type.148, f32[2048]{0:T(1024)S(1)} %fusion.38, f32[2048,768]{1,0:T(8,128)} %copy-done.2, f32[2048]{0:T(1024)S(1)} %broadcast_multiply_fusion.1, ...), kind=kOutput, calls=%fused_computation.132 | convolution fusion | flops 9676257280 | bytes 42501120 | tf_op jit(solution)/shard_map/dot_general | solution.py:137
  304.6 0.9 multiply_reduce_fusion.6
  305.5 1.4 multiply_convert_fusion.2
  307.1 1.7 copy-done.11
  308.9 7.1 all-gather.15.cloned.1.call-done
  316.0 1.7 multiply_reduce_fusion.9
  318.6 54.8 %all-gather.17.cloned.1.call-done = bf16[1024,768]{1,0:T(8,128)(2,1)} async-done(((bf16[32,768]{1,0:T(8,128)(2,1)}), bf16[1024,768]{1,0:T(8,128)(2,1)}) %all-gather.17.cloned.1.call-update) | async-done | bytes 1572880 | tf_op jit(solution)/shard_map/all_gather | solution.py:156
  373.3 2.1 fusion.61
  376.2 2.4 fusion.35
  378.7 5.5 convert_element_type.161
  384.7 94.7 %reduce-scatter.9.cloned.1.call-done = f32[32,768]{1,0:T(8,128)} async-done(((f32[1024,768]{1,0:T(8,128)}), f32[32,768]{1,0:T(8,128)}) %reduce-scatter.9.cloned.1.call-update) | async-done | bytes 98320 | tf_op jit(solution)/shard_map/reduce_scatter | solution.py:182
  479.4 1.0 multiply_reduce_fusion.8
  480.4 1.6 convert_reduce_fusion.4
  482.0 2.0 fusion.65
  484.6 1.8 slice_add_fusion
  486.3 5.2 scatter-add.4
  491.6 11.6 multiply_reduce_fusion.2
  503.3 3.7 fusion.52
  506.9 6.3 convert_reduce_fusion.2
  513.3 29.3 %convert_reduce_fusion.1 = (f32[3072]{0:T(1024)}, bf16[2048,3072]{1,0:T(8,128)(2,1)}) fusion(f32[2048,3072]{1,0:T(8,128)} %get-tuple-element.132, bf16[2048,768]{1,0:T(8,128)(2,1)S(1)} %get-tuple-element.118, bf16[3072,768]{1,0:T(8,128)(2,1)} %all-gather.13.cloned.1.call-done, f32[2048,3072]{1,0:T(8,128)} %get-tuple-element.147, ...), kind=kOutput, calls=%fused_computation.5 | convolution fusion | flops 9770628096 | bytes 70803456 | tf_op jit(solution)/shard_map/dot_general | solution.py:33
  542.6 19.7 %multiply_reduce_fusion.3 = (f32[768]{0:T(1024)}, f32[2048]{0:T(1024)S(1)}, f32[768]{0:T(1024)}, f32[2048,768]{1,0:T(8,128)S(1)}) fusion(f32[2048,768]{1,0:T(8,128)} %copy-done.2, f32[2048]{0:T(1024)S(1)} %fusion.38, f32[2048]{0:T(1024)S(1)} %broadcast_multiply_fusion.1, f32[768]{0:T(1024)S(1)} %convert_element_type.148, ...), kind=kOutput, calls=%fused_computation.50 | convolution fusion | flops 9679400960 | bytes 36217856 | tf_op jit(solution)/shard_map/dot_general | solution.py:33
  562.3 4.2 fusion.51
  566.6 6.3 convert_reduce_fusion.3
  572.9 1.7 copy-done.13
  574.5 2.9 convolution_convert_fusion
  577.4 7.2 reshape.281
  584.6 17.4 %multiply_reduce_fusion = (f32[64,12,32]{2,1,0:T(8,128)S(1)}, f32[64,12,32,32]{2,3,1,0:T(8,128)}) fusion(f32[64,12,32,32]{2,3,1,0:T(8,128)} %get-tuple-element.145, f32[64,12,32]{2,1,0:T(8,128)} %copy-done.16, bf16[64,32,1,12,64]{4,3,2,1,0:T(8,128)(2,1)} %get-tuple-element.137, bf16[64,32,12,64]{3,2,1,0:T(8,128)(2,1)} %reshape.281), kind=kOutput, calls=%fused_computation.25 | convolution fusion | flops 102998016 | bytes 12779520 | tf_op jit(solution)/shard_map/sqhe,skhe->shqk/dot_general | solution.py:229
  602.0 10.1 multiply_convert_fusion.1
  612.2 9.7 multiply_bitcast_fusion.1
  621.9 4.1 fusion.63
  626.0 9.7 multiply_bitcast_fusion
  635.6 11.2 fusion.27
  646.9 12.6 %convert_reduce_fusion = (f32[3,12,64]{2,1,0:T(8,128)S(1)}, bf16[64,32,3,12,64]{4,1,3,0,2:T(8,128)(2,1)S(1)}) fusion(bf16[64,32,1,12,64]{4,1,3,0,2:T(8,128)(2,1)} %fusion.27, bf16[64,32,1,12,64]{4,1,3,0,2:T(8,128)(2,1)} %multiply_bitcast_fusion, bf16[64,32,1,12,64]{4,1,3,0,2:T(8,128)(2,1)} %multiply_bitcast_fusion.1), kind=kLoop, calls=%fused_computation.3 | loop fusion | flops 18872064 | bytes 18883584 | tf_op jit(solution)/shard_map/reduce_sum | solution.py:39
  659.5 13.1 %copy.68 = bf16[64,32,3,12,64]{4,3,2,1,0:T(8,128)(2,1)} copy(bf16[64,32,3,12,64]{4,1,3,0,2:T(8,128)(2,1)S(1)} %get-tuple-element.122) | data formatting | bytes 18874368 | tf_op jit(solution)/shard_map/convert_element_type | solution.py:246
  672.6 30.4 %convert_element_type.171 = bf16[2048,2304]{1,0:T(8,128)(2,1)} reshape(bf16[64,32,3,12,64]{4,3,2,1,0:T(8,128)(2,1)} %copy.68) | data formatting | bytes 18874368 | tf_op jit(solution)/shard_map/convert_element_type | solution.py:246
  703.1 12.0 %convolution_bitcast_fusion = f32[768,2304]{0,1:T(8,128)} fusion(bf16[2048,2304]{1,0:T(8,128)(2,1)} %convert_element_type.171, bf16[2048,768]{1,0:T(8,128)(2,1)S(1)} %bitcast.109), kind=kOutput, calls=%fused_computation.69 | convolution fusion | flops 7247757312 | bytes 19660800 | tf_op jit(solution)/shard_map/dot_general | solution.py:27
  715.1 8.0 copy.72
  723.2 16.2 %fusion.64 = f32[3072,768]{1,0:T(8,128)} fusion(bf16[2048,3072]{1,0:T(8,128)(2,1)} %get-tuple-element.131, bf16[2048,768]{1,0:T(8,128)(2,1)} %copy-done.12), kind=kOutput, calls=%fused_computation.141 | convolution fusion | flops 9663676416 | bytes 25165824 | tf_op jit(solution)/shard_map/dot_general | solution.py:27
  740.1 18.4 %fusion.44 = f32[768,3072]{1,0:T(8,128)} fusion(bf16[2048,3072]{1,0:T(8,128)(2,1)} %get-tuple-element.157, f32[2048,768]{1,0:T(8,128)} %copy-done.2, f32[768]{0:T(1024)S(1)} %copy-done.36, f32[768]{0:T(1024)S(1)} %convert_element_type.148, f32[2048]{0:T(1024)S(1)} %fusion.38, f32[2048]{0:T(1024)S(1)} %broadcast_multiply_fusion.1), kind=kOutput, calls=%fused_computation.128 | convolution fusion | flops 9671540736 | bytes 28334080 | tf_op jit(solution)/shard_map/dot_general | solution.py:27
  760.6 5.5 multiply_reduce_fusion.1
  766.1 2.0 pad_maximum_fusion.3
  768.2 41.0 %all-reduce.18 = (f32[]{:T(128)}, f32[4]{0:T(128)S(1)}, f32[1536]{0:T(1024)S(1)}, f32[768]{0:T(1024)S(1)}, f32[768]{0:T(1024)S(1)}, /*index=5*/f32[768]{0:T(1024...) all-reduce(f32[]{:T(128)} %get-tuple-element.127, ...), channel_id=1, replica_groups=mesh['fsdp'=8,'dp'=4] {'fsdp','dp'}, use_global_device_ids=true, to_apply=%region_11.12 | all-reduce | flops 9989 | bytes 79912 | tf_op jit(solution)/shard_map/psum | solution.py:175
  816.9 13.6 %add_convert_fusion.2 = bf16[2048,768]{1,0:T(8,128)(2,1)} fusion(f32[2048,768]{1,0:T(8,128)} %copy-done.4, bf16[2048,2304]{1,0:T(8,128)(2,1)} %convert_element_type.171, bf16[768,2304]{1,0:T(8,128)(2,1)} %all-gather.7.cloned.1.call-done, f32[2048]{0:T(1024)S(1)} %copy-done.25), kind=kOutput, calls=%fused_computation.52 | convolution fusion | flops 7252475904 | bytes 22421504 | tf_op jit(solution)/shard_map/dot_general | solution.py:33
  830.5 39.3 %reduce-scatter.19.cloned.1.call-done = f32[24,2304]{1,0:T(8,128)} async-done(((f32[768,2304]{1,0:T(8,128)}), f32[24,2304]{1,0:T(8,128)}) %reduce-scatter.19.cloned.1.call-update) | async-done | bytes 221200
  869.8 142.3 %reduce-scatter.15.cloned.1.call-done = f32[96,768]{1,0:T(8,128)} async-done(((f32[3072,768]{1,0:T(8,128)}), f32[96,768]{1,0:T(8,128)}) %reduce-scatter.15.cloned.1.call-update) | async-done | bytes 294928 | tf_op jit(solution)/shard_map/reduce_scatter | solution.py:209
  1012.1 141.0 %reduce-scatter.13.cloned.1.call-done = f32[24,3072]{1,0:T(8,128)} async-done(((f32[768,3072]{1,0:T(8,128)}), f32[24,3072]{1,0:T(8,128)}) %reduce-scatter.13.cloned.1.call-update) | async-done | bytes 294928 | tf_op jit(solution)/shard_map/reduce_scatter | solution.py:207
  (176 shorter events, 24.7 us)
Async XLA Ops:
  7.2 71.1 %all-gather.7.cloned.1.call-start = ((), (), s32[]{:S(2)}) async-start(), calls=%async_computation.6 | async-start | bytes 3649536 | tf_op jit(solution)/shard_map/all_gather | solution.py:70
  7.9 192.5 %all-gather.9.cloned.1.call-start = ((), (), s32[]{:S(2)}) async-start(), calls=%async_computation.7 | async-start | bytes 1216512 | tf_op jit(solution)/shard_map/all_gather | solution.py:72
  8.7 206.0 %all-gather.11.cloned.1.call-start = ((), (), s32[]{:S(2)}) async-start(), calls=%async_computation.8 | async-start | bytes 4866048 | tf_op jit(solution)/shard_map/all_gather | solution.py:123
  9.4 275.5 %all-gather.13.cloned.1.call-start = ((), (), s32[]{:S(2)}) async-start(), calls=%async_computation.9 | async-start | bytes 4866048 | tf_op jit(solution)/shard_map/all_gather | solution.py:125
  10.0 306.0 %all-gather.15.cloned.1.call-start = ((), (), s32[]{:S(2)}) async-start(), calls=%async_computation.10 | async-start | bytes 1216512 | tf_op jit(solution)/shard_map/all_gather | solution.py:129
  10.6 362.7 %all-gather.17.cloned.1.call-start = ((), (), s32[]{:S(2)}) async-start(), calls=%async_computation.11 | async-start | bytes 1622016 | tf_op jit(solution)/shard_map/all_gather | solution.py:156
  61.5 15.5 %copy-start.18 = (f32[32,32]{1,0:T(8,128)}, f32[32,32]{1,0:T(8,128)S(1)}, u32[]{:S(2)}) copy-start(f32[32,32]{1,0:T(8,128)S(1)} %get-tuple-element.142) | copy-start | bytes 12292
  68.2 216.6 %copy-start.35 = (f32[768]{0:T(1024)}, f32[768]{0:T(1024)S(1)}, u32[]{:S(2)}) copy-start(f32[768]{0:T(1024)S(1)} %convert_element_type.149) | copy-start | bytes 9220
  68.8 9.5 copy-start.6
  166.1 11.4 copy-start.16
  210.6 2.6 copy-start.2
  214.1 0.6 copy-start.21
  214.7 70.2 %copy-start.37 = (f32[768]{0:T(1024)S(1)}, f32[768]{0:T(1024)}, u32[]{:S(2)}) copy-start(f32[768]{0:T(1024)} %convert_element_type.153) | copy-start | bytes 9220
  304.5 2.6 copy-start.1
  304.5 0.9 copy-start.20
  304.5 0.9 copy-start.23
  304.5 0.9 copy-start.29
  305.4 10.6 copy-start.28
  307.1 1.7 copy-start.11
  318.5 160.9 %reduce-scatter.9.cloned.1.call-start = ((), (), s32[]{:S(2)}) async-start(), calls=%async_computation.12 | async-start | bytes 3244032 | tf_op jit(solution)/shard_map/reduce_scatter | solution.py:182
  378.6 5.6 copy-start.9
  378.7 105.4 %copy-start.10 = (bf16[768,768]{1,0:T(8,128)(2,1)S(1)}, bf16[768,768]{1,0:T(8,128)(2,1)}, u32[]{:S(2)}) copy-start(bf16[768,768]{1,0:T(8,128)(2,1)} %all-gather.15.cloned.1.call-done) | copy-start | bytes 3538948
  378.7 451.8 %reduce-scatter.17.cloned.1.call-start = ((), (), s32[]{:S(2)}) async-start(), calls=%async_computation.16 | async-start | bytes 2433024 | tf_op jit(solution)/shard_map/reduce_scatter | solution.py:213
  484.0 346.5 %reduce-scatter.11.cloned.1.call-start = ((), (), s32[]{:S(2)}) async-start(), calls=%async_computation.13 | async-start | bytes 2433024 | tf_op jit(solution)/shard_map/reduce_scatter | solution.py:262
  484.6 18.6 %slice-start = ((s8[6291456]{0:T(1024)(128)(4,1)}), s8[2097152]{0:T(1024)(128)(4,1)S(1)}, s32[]{:S(2)}) async-start(s8[6291456]{0:T(1024)(128)(4,1)} %bitcast.106), calls=%async_computation.18 | async-start | bytes 4194304
  491.6 11.6 copy-start
  491.6 11.7 %slice-start.1 = ((s8[6291456]{0:T(1024)(128)(4,1)}), s8[4194304]{0:T(1024)(128)(4,1)S(1)}, s32[]{:S(2)}) async-start(s8[6291456]{0:T(1024)(128)(4,1)} %bitcast.106), calls=%async_computation.19 | async-start | bytes 8388608
  506.9 6.3 copy-start.5
  513.3 29.3 %copy-start.12 = (bf16[2048,768]{1,0:T(8,128)(2,1)}, bf16[2048,768]{1,0:T(8,128)(2,1)S(1)}, u32[]{:S(2)}) copy-start(bf16[2048,768]{1,0:T(8,128)(2,1)S(1)} %get-tuple-element.118) | copy-start | bytes 9437188
  542.6 19.7 %copy-start.22 = (f32[2048]{0:T(1024)S(1)}, f32[2048]{0:T(1024)}, u32[]{:S(2)}) copy-start(f32[2048]{0:T(1024)} %copy-done.21) | copy-start | bytes 24580
  566.5 6.3 copy-start.4
  566.5 6.3 copy-start.24
  566.6 8.0 copy-start.15
  572.9 1.7 copy-start.13
  584.6 17.4 %copy-start.17 = (f32[64,12,32]{2,1,0:T(8,128)S(1)}, f32[64,12,32]{2,1,0:T(8,128)}, u32[]{:S(2)}) copy-start(f32[64,12,32]{2,1,0:T(8,128)} %copy-done.16) | copy-start | bytes 294916
  612.2 9.7 copy-start.3
  612.2 9.7 copy-start.8
  612.2 9.7 copy-start.14
  646.9 222.9 %reduce-scatter.19.cloned.1.call-start = ((), (), s32[]{:S(2)}) async-start(), calls=%async_computation.17 | async-start | bytes 7299072
  672.6 30.4 %copy-start.7 = (bf16[2,32,32,768]{3,2,1,0:T(8,128)(2,1)S(1)}, bf16[2,32,32,768]{3,2,1,0:T(8,128)(2,1)}, u32[]{:S(2)}) copy-start(bf16[2,32,32,768]{3,2,1,0:T(8,128)(2,1)} %param.21) | copy-start | bytes 9437188
  723.1 288.9 %reduce-scatter.15.cloned.1.call-start = ((), (), s32[]{:S(2)}) async-start(), calls=%async_computation.15 | async-start | bytes 9732096 | tf_op jit(solution)/shard_map/reduce_scatter | solution.py:209
  739.4 0.7 copy-start.36
  739.4 413.6 %reduce-scatter.13.cloned.1.call-start = ((), (), s32[]{:S(2)}) async-start(), calls=%async_computation.14 | async-start | bytes 9732096 | tf_op jit(solution)/shard_map/reduce_scatter | solution.py:207
  758.5 0.7 copy-start.38
  758.5 2.2 copy-start.19
  759.1 9.0 copy-start.26
  759.2 9.0 copy-start.27
  759.2 9.0 copy-start.30
  759.2 9.0 copy-start.31
  759.2 9.0 copy-start.32
  759.2 9.0 copy-start.33
  759.2 9.0 copy-start.34
  759.2 57.7 %copy-start.25 = (f32[2048]{0:T(1024)S(1)}, f32[2048]{0:T(1024)}, u32[]{:S(2)}) copy-start(f32[2048]{0:T(1024)} %copy-done.24) | copy-start | bytes 24580
Sparse Core Ops, SparseCore 0:
  10.9 63.0 all-gather.6
  76.9 52.8 all-gather.8
  132.7 62.4 all-gather.10
  198.0 62.3 all-gather.12
  263.1 52.8 all-gather.14
  319.3 53.9 all-gather.16
  378.8 100.5 reduce-scatter.8
  485.2 97.9 reduce-scatter.16
  647.0 97.9 reduce-scatter.10
  751.1 118.6 reduce-scatter.18
  877.3 134.7 reduce-scatter.14
  1018.4 134.5 reduce-scatter.12
where the time goes:
time: 1170 us; the launch traced here: 1160 us
  waiting for transfers between devices  482 us (41%)
  matrix products  310 us (26%)
  local copies, waits for them, and re-layouts  156 us (13%)
  other arithmetic  111 us (9%)
  blocking collectives  83.6 us (7%)
  between operations  18.3 us (2%)
    reduce_scatter x1, waiting for transfers between devices, on_device(): lax.psum_scatter(grad_narrow_weight, ('fsdp', 'dp'), scatter_dimension=0,...  142 us
    reduce_scatter x1, waiting for transfers between devices, on_device(): lax.psum_scatter(grad_widen_weight, ('fsdp', 'dp'), scatter_dimension=0,...  141 us
    reduce_scatter x1, waiting for transfers between devices, on_device(): lax.psum_scatter(dsecond_all, ('fsdp', 'dp'), scatter_dimension=0, tiled=...  94.7 us
    dot_general x1, matrix products, on_device(): jnp.dot(hidden_low, widen, preferred_element_type=jnp.float32)  70.2 us
    dot_general x6, matrix products, times_transpose(): lax.dot_general(left_side, right_side, (((1,), (1,)), ((), ())), preferre...  68 us
    dot_general x6, matrix products, rows_product(): lax.dot_general(left_side, right_side, (((0,), (0,)), ((), ())), preferre...  55.1 us
    all_gather x1, waiting for transfers between devices, on_device(): lax.all_gather(second_unit, ('fsdp', 'dp'), axis=0, tiled=True)  54.8 us
    convert_element_type x2, local copies, waits for them, and re-layouts, on_device(): dpacked = jnp.stack([dqueries, dkey_rows, dvalues], axis=2).astype(jnp.bf...  43.5 us
  transfers between devices with their start and end apart: 12, of which 6 were waited for; matrix products, arithmetic and copies ran while one was open for 48% of the time, Pallas kernels for 0%

commit v1 on v0

--- a/solution.py
+++ b/solution.py
@@ -6,6 +6,11 @@
 HEADS = 12
 DROP_SCALE = 1.0 / 0.9
 SOFTMAX_TEMP = 0.05
+
+
+def by_each_axis(array, inner_axis, outer_axis):
+    partial = lax.psum(array, inner_axis)
+    return lax.psum(partial, outer_axis)
 
 
 def layer_norm(values, norm_gain, norm_shift):
@@ -172,7 +177,7 @@
             2.0 * jnp.sum(sent_lengths).astype(jnp.float32),
         ]
     )
-    loss_total, sums_total = lax.psum((loss_part, square_sums), ("fsdp", "dp"))
+    loss_total, sums_total = by_each_axis((loss_part, square_sums), "dp", "fsdp")
     loss_value = loss_total / sentence_total
     rms_stats = jnp.sqrt(sums_total[:3] / (sums_total[3] * model_width))
     softmax_probs = jnp.exp(scaled_logits - log_total[:, None])

time: 1170 us -> 1170 us (level)
  blocking collectives: 83.6 us -> 106 us
  waiting for transfers between devices: 482 us -> 460 us
    unnamed x1 -> x2, blocking collectives: 42.6 us -> 81.7 us
    unnamed x13, waiting for transfers between devices: 42.5 us -> 19.8 us
    psum x1 -> x2, blocking collectives: 41 us -> 24.3 us  [the longest x1 14.2 us: by_each_axis(): return lax.psum(partial, outer_axis)]
where the time goes in v1:
time: 1170 us; the launch traced here: 1160 us
  waiting for transfers between devices  460 us (39%)
  matrix products  310 us (26%)
  local copies, waits for them, and re-layouts  156 us (13%)
  other arithmetic  111 us (9%)
  blocking collectives  106 us (9%)
  between operations  18.3 us (2%)
    reduce_scatter x1, waiting for transfers between devices, on_device(): lax.psum_scatter(grad_narrow_weight, ('fsdp', 'dp'), scatter_dimension=0,...  142 us
    reduce_scatter x1, waiting for transfers between devices, on_device(): lax.psum_scatter(grad_widen_weight, ('fsdp', 'dp'), scatter_dimension=0,...  141 us
    reduce_scatter x1, waiting for transfers between devices, on_device(): lax.psum_scatter(dsecond_all, ('fsdp', 'dp'), scatter_dimension=0, tiled=...  94.6 us
    unnamed x2, blocking collectives  81.7 us
    dot_general x1, matrix products, on_device(): jnp.dot(hidden_low, widen, preferred_element_type=jnp.float32)  70.2 us
    dot_general x6, matrix products, times_transpose(): lax.dot_general(left_side, right_side, (((1,), (1,)), ((), ())), preferre...  67.7 us
    dot_general x6, matrix products, rows_product(): lax.dot_general(left_side, right_side, (((0,), (0,)), ((), ())), preferre...  55.1 us
    all_gather x1, waiting for transfers between devices, on_device(): lax.all_gather(second_unit, ('fsdp', 'dp'), axis=0, tiled=True)  54.8 us
  transfers between devices with their start and end apart: 12, of which 6 were waited for; matrix products, arithmetic and copies ran while one was open for 48% of the time, Pallas kernels for 0%

profile of v1, /device:TPU:0, one launch (start us, length us, event | category | flops | bytes accessed | tf_op | source)
XLA Modules:
  0.0 1160.9 jit_solution(715993819725513326)
XLA Ops:
  10.6 0.8 dynamic-update-slice.10
  16.5 0.8 dynamic-update-slice.7
  18.2 42.6 %all-reduce.21 = (bf16[1536]{0:T(1024)(128)(2,1)S(1)}, bf16[768]{0:T(1024)(128)(2,1)S(1)}, bf16[768]{0:T(1024)(128)(2,1)S(1)}, bf16[768]{0:T(1024)(128)(2,1)S(1)...) all-reduce(bf16[1536]{0:T(1024)(128)(2,1)S(1)} %dynamic-update-slic, ...), channel_id=1, replica_groups=mesh['fsdp'=8,'dp'=4] {'fsdp','dp'}, use_global_device_ids=true, to_apply=%add | all-reduce | flops 9984 | bytes 39936
  61.5 6.7 convert_multiply_fusion.1
  68.8 7.0 convert_multiply_fusion
  78.3 11.8 %add_convert_fusion.1 = bf16[2048,2304]{1,0:T(8,128)(2,1)} fusion(bf16[2048,768]{1,0:T(8,128)(2,1)S(1)} %bitcast.108, bf16[768,2304]{1,0:T(8,128)(2,1)} %all-gather.7.cloned.1.call-done, f32[2304]{0:T(1024)S(1)} %pad_maximum_fusion.1), kind=kOutput, calls=%fused_computation.21 | convolution fusion | flops 7257194496 | bytes 16131072 | tf_op jit(solution)/shard_map/dot_general | solution.py:99
  90.1 28.7 %reshape.277 = bf16[64,32,3,12,64]{4,3,2,1,0:T(8,128)(2,1)} reshape(bf16[2048,2304]{1,0:T(8,128)(2,1)} %add_convert_fusion.1) | data formatting | bytes 18874368 | tf_op jit(solution)/shard_map/reshape | solution.py:102
  118.8 17.1 %fusion.57 = (bf16[64,32,1,12,64]{4,3,2,1,0:T(8,128)(2,1)}, bf16[64,32,1,12,64]{4,3,2,1,0:T(8,128)(2,1)}, bf16[64,32,1,12,64]{4,3,2,1,0:T(8,128)(2,1)}) fusion(bf16[64,32,3,12,64]{4,3,2,1,0:T(8,128)(2,1)} %reshape.277), kind=kLoop, calls=%fused_computation.134 | loop fusion | bytes 18874368 | tf_op jit(solution)/shard_map/slice | solution.py:104
  136.0 13.9 %fusion.22 = f32[64,12,32,32]{2,3,1,0:T(8,128)} fusion(bf16[64,32,1,12,64]{4,3,2,1,0:T(8,128)(2,1)} %get-tuple-element.138, bf16[64,32,1,12,64]{4,3,2,1,0:T(8,128)(2,1)} %get-tuple-element.137), kind=kOutput, calls=%fused_computation.75 | convolution fusion | flops 100663296 | bytes 9437184 | tf_op jit(solution)/shard_map/sqhe,skhe->shqk/dot_general | solution.py:107
  149.9 16.3 %fusion.60 = (f32[64,12,32]{2,1,0:T(8,128)S(1)}, f32[64,12,32,32]{2,3,1,0:T(8,128)}) fusion(f32[64,12,32,32]{2,3,1,0:T(8,128)} %fusion.22, pred[64,32]{1,0:T(8,128)(4,1)S(1)} %bitcast.115), kind=kOutput, calls=%fused_computation.137 | output fusion | flops 4718623 | bytes 6391808 | tf_op jit(solution)/shard_map/sub | solution.py:111
  166.1 11.4 convert_bitcast_fusion
  177.5 11.3 copy.62
  188.8 11.5 convert_element_type.145
  200.4 10.2 fusion.56
  210.6 2.6 copy-done.2
  214.7 70.2 %multiply_convert_fusion = (bf16[2048,3072]{1,0:T(8,128)(2,1)}, f32[2048,3072]{1,0:T(8,128)}, f32[2048,3072]{1,0:T(8,128)}) fusion(f32[3072]{0:T(1024)S(1)} %convert_element_type.151, bf16[768,3072]{1,0:T(8,128)(2,1)} %all-gather.11.cloned.1.call-done, f32[2048,768]{1,0:T(8,128)} %copy-done.2, f32[768]{0:T(1024)S(1)} %convert_element_type.149, ...), kind=kOutput, calls=%fused_computation.7 | convolution fusion | flops 10086776832 | bytes 73959424 | tf_op jit(solution)/shard_map/dot_general | solution.py:137
  284.9 19.6 %fusion.53 = (f32[2048]{0:T(1024)S(1)}, f32[2048,768]{1,0:T(8,128)S(1)}, f32[2048,768]{1,0:T(8,128)}) fusion(f32[768]{0:T(1024)S(1)} %convert_element_type.149, f32[768]{0:T(1024)S(1)} %convert_element_type.148, f32[2048]{0:T(1024)S(1)} %fusion.38, f32[2048,768]{1,0:T(8,128)} %copy-done.2, f32[2048]{0:T(1024)S(1)} %broadcast_multiply_fusion.1, ...), kind=kOutput, calls=%fused_computation.132 | convolution fusion | flops 9676257280 | bytes 42501120 | tf_op jit(solution)/shard_map/dot_general | solution.py:142
  304.6 0.9 multiply_reduce_fusion.6
  305.5 1.4 multiply_convert_fusion.2
  307.1 1.7 copy-done.11
  308.9 7.1 all-gather.15.cloned.1.call-done
  316.0 1.7 multiply_reduce_fusion.9
  318.6 54.8 %all-gather.17.cloned.1.call-done = bf16[1024,768]{1,0:T(8,128)(2,1)} async-done(((bf16[32,768]{1,0:T(8,128)(2,1)}), bf16[1024,768]{1,0:T(8,128)(2,1)}) %all-gather.17.cloned.1.call-update) | async-done | bytes 1572880 | tf_op jit(solution)/shard_map/all_gather | solution.py:161
  373.3 2.1 fusion.61
  376.3 2.4 fusion.35
  378.7 5.5 convert_element_type.161
  384.7 94.6 %reduce-scatter.9.cloned.1.call-done = f32[32,768]{1,0:T(8,128)} async-done(((f32[1024,768]{1,0:T(8,128)}), f32[32,768]{1,0:T(8,128)}) %reduce-scatter.9.cloned.1.call-update) | async-done | bytes 98320 | tf_op jit(solution)/shard_map/reduce_scatter | solution.py:187
  479.3 1.0 multiply_reduce_fusion.8
  480.4 1.6 convert_reduce_fusion.4
  482.0 2.0 fusion.65
  484.5 1.8 slice_add_fusion
  486.3 5.2 scatter-add.4
  491.5 11.6 multiply_reduce_fusion.2
  503.2 3.7 fusion.52
  506.9 6.3 convert_reduce_fusion.2
  513.2 29.3 %convert_reduce_fusion.1 = (f32[3072]{0:T(1024)}, bf16[2048,3072]{1,0:T(8,128)(2,1)}) fusion(f32[2048,3072]{1,0:T(8,128)} %get-tuple-element.134, bf16[2048,768]{1,0:T(8,128)(2,1)S(1)} %get-tuple-element.120, bf16[3072,768]{1,0:T(8,128)(2,1)} %all-gather.13.cloned.1.call-done, f32[2048,3072]{1,0:T(8,128)} %get-tuple-element.149, ...), kind=kOutput, calls=%fused_computation.5 | convolution fusion | flops 9770628096 | bytes 70803456 | tf_op jit(solution)/shard_map/dot_general | solution.py:38
  542.5 19.7 %multiply_reduce_fusion.3 = (f32[768]{0:T(1024)}, f32[2048]{0:T(1024)S(1)}, f32[768]{0:T(1024)}, f32[2048,768]{1,0:T(8,128)S(1)}) fusion(f32[2048,768]{1,0:T(8,128)} %copy-done.2, f32[2048]{0:T(1024)S(1)} %fusion.38, f32[2048]{0:T(1024)S(1)} %broadcast_multiply_fusion.1, f32[768]{0:T(1024)S(1)} %convert_element_type.148, ...), kind=kOutput, calls=%fused_computation.50 | convolution fusion | flops 9679400960 | bytes 36217856 | tf_op jit(solution)/shard_map/dot_general | solution.py:38
  562.2 4.2 fusion.51
  566.5 6.3 convert_reduce_fusion.3
  572.8 1.7 copy-done.13
  574.5 2.9 convolution_convert_fusion
  577.4 7.2 reshape.281
  584.6 17.4 %multiply_reduce_fusion = (f32[64,12,32]{2,1,0:T(8,128)S(1)}, f32[64,12,32,32]{2,3,1,0:T(8,128)}) fusion(f32[64,12,32,32]{2,3,1,0:T(8,128)} %get-tuple-element.147, f32[64,12,32]{2,1,0:T(8,128)} %copy-done.16, bf16[64,32,1,12,64]{4,3,2,1,0:T(8,128)(2,1)} %get-tuple-element.139, bf16[64,32,12,64]{3,2,1,0:T(8,128)(2,1)} %reshape.281), kind=kOutput, calls=%fused_computation.25 | convolution fusion | flops 102998016 | bytes 12779520 | tf_op jit(solution)/shard_map/sqhe,skhe->shqk/dot_general | solution.py:234
  602.0 10.1 multiply_convert_fusion.1
  612.2 9.7 multiply_bitcast_fusion.1
  621.9 4.1 fusion.63
  626.0 9.7 multiply_bitcast_fusion
  635.6 11.2 fusion.27
  646.9 12.6 %convert_reduce_fusion = (f32[3,12,64]{2,1,0:T(8,128)S(1)}, bf16[64,32,3,12,64]{4,1,3,0,2:T(8,128)(2,1)S(1)}) fusion(bf16[64,32,1,12,64]{4,1,3,0,2:T(8,128)(2,1)} %fusion.27, bf16[64,32,1,12,64]{4,1,3,0,2:T(8,128)(2,1)} %multiply_bitcast_fusion, bf16[64,32,1,12,64]{4,1,3,0,2:T(8,128)(2,1)} %multiply_bitcast_fusion.1), kind=kLoop, calls=%fused_computation.3 | loop fusion | flops 18872064 | bytes 18883584 | tf_op jit(solution)/shard_map/reduce_sum | solution.py:44
  659.5 13.1 %copy.68 = bf16[64,32,3,12,64]{4,3,2,1,0:T(8,128)(2,1)} copy(bf16[64,32,3,12,64]{4,1,3,0,2:T(8,128)(2,1)S(1)} %get-tuple-element.124) | data formatting | bytes 18874368 | tf_op jit(solution)/shard_map/convert_element_type | solution.py:251
  672.6 30.4 %convert_element_type.171 = bf16[2048,2304]{1,0:T(8,128)(2,1)} reshape(bf16[64,32,3,12,64]{4,3,2,1,0:T(8,128)(2,1)} %copy.68) | data formatting | bytes 18874368 | tf_op jit(solution)/shard_map/convert_element_type | solution.py:251
  703.1 12.0 %convolution_bitcast_fusion = f32[768,2304]{0,1:T(8,128)} fusion(bf16[2048,2304]{1,0:T(8,128)(2,1)} %convert_element_type.171, bf16[2048,768]{1,0:T(8,128)(2,1)S(1)} %bitcast.109), kind=kOutput, calls=%fused_computation.69 | convolution fusion | flops 7247757312 | bytes 19660800 | tf_op jit(solution)/shard_map/dot_general | solution.py:32
  715.1 8.0 copy.72
  723.2 16.2 %fusion.64 = f32[3072,768]{1,0:T(8,128)} fusion(bf16[2048,3072]{1,0:T(8,128)(2,1)} %get-tuple-element.133, bf16[2048,768]{1,0:T(8,128)(2,1)} %copy-done.12), kind=kOutput, calls=%fused_computation.141 | convolution fusion | flops 9663676416 | bytes 25165824 | tf_op jit(solution)/shard_map/dot_general | solution.py:32
  740.1 18.4 %fusion.44 = f32[768,3072]{1,0:T(8,128)} fusion(bf16[2048,3072]{1,0:T(8,128)(2,1)} %get-tuple-element.159, f32[2048,768]{1,0:T(8,128)} %copy-done.2, f32[768]{0:T(1024)S(1)} %copy-done.36, f32[768]{0:T(1024)S(1)} %convert_element_type.148, f32[2048]{0:T(1024)S(1)} %fusion.38, f32[2048]{0:T(1024)S(1)} %broadcast_multiply_fusion.1), kind=kOutput, calls=%fused_computation.128 | convolution fusion | flops 9671540736 | bytes 28334080 | tf_op jit(solution)/shard_map/dot_general | solution.py:32
  760.4 5.5 multiply_reduce_fusion.1
  765.9 2.0 pad_maximum_fusion.3
  767.9 10.1 all-reduce.20
  778.1 14.2 %all-reduce.19 = (f32[]{:T(128)}, f32[4]{0:T(128)S(1)}) all-reduce(f32[]{:T(128)} %get-tuple-element.106, f32[4]{0:T(128)S(1)} %get-tuple-element.107), channel_id=1, replica_groups=mesh['fsdp'=8,'dp'=4] {'fsdp'}, use_global_device_ids=true, to_apply=%region_12.13 | all-reduce | flops 5 | bytes 40 | tf_op jit(solution)/shard_map/psum | solution.py:13
  792.5 39.2 %all-reduce.18 = (f32[1536]{0:T(1024)S(1)}, f32[768]{0:T(1024)S(1)}, f32[768]{0:T(1024)S(1)}, f32[768]{0:T(1024)S(1)}, f32[3072]{0:T(1024)S(1)}, /*index=5*/f32[...) all-reduce(f32[1536]{0:T(1024)S(1)} %pad_maximum_fusion.2, ...), channel_id=4, replica_groups=mesh['fsdp'=8,'dp'=4] {'fsdp','dp'}, use_global_device_ids=true, to_apply=%region_28.29.clone | all-reduce | flops 9984 | bytes 79872
  839.3 13.2 %add_convert_fusion.2 = bf16[2048,768]{1,0:T(8,128)(2,1)} fusion(f32[2048,768]{1,0:T(8,128)} %copy-done.4, bf16[2048,2304]{1,0:T(8,128)(2,1)} %convert_element_type.171, bf16[768,2304]{1,0:T(8,128)(2,1)} %all-gather.7.cloned.1.call-done, f32[2048]{0:T(1024)S(1)} %copy-done.25), kind=kOutput, calls=%fused_computation.52 | convolution fusion | flops 7252475904 | bytes 22421504 | tf_op jit(solution)/shard_map/dot_general | solution.py:38
  852.6 16.6 %reduce-scatter.19.cloned.1.call-done = f32[24,2304]{1,0:T(8,128)} async-done(((f32[768,2304]{1,0:T(8,128)}), f32[24,2304]{1,0:T(8,128)}) %reduce-scatter.19.cloned.1.call-update) | async-done | bytes 221200
  869.2 142.3 %reduce-scatter.15.cloned.1.call-done = f32[96,768]{1,0:T(8,128)} async-done(((f32[3072,768]{1,0:T(8,128)}), f32[96,768]{1,0:T(8,128)}) %reduce-scatter.15.cloned.1.call-update) | async-done | bytes 294928 | tf_op jit(solution)/shard_map/reduce_scatter | solution.py:214
  1011.5 141.0 %reduce-scatter.13.cloned.1.call-done = f32[24,3072]{1,0:T(8,128)} async-done(((f32[768,3072]{1,0:T(8,128)}), f32[24,3072]{1,0:T(8,128)}) %reduce-scatter.13.cloned.1.call-update) | async-done | bytes 294928 | tf_op jit(solution)/shard_map/reduce_scatter | solution.py:212
  (178 shorter events, 26.3 us)
Async XLA Ops:
  7.2 71.1 %all-gather.7.cloned.1.call-start = ((), (), s32[]{:S(2)}) async-start(), calls=%async_computation.6 | async-start | bytes 3649536 | tf_op jit(solution)/shard_map/all_gather | solution.py:75
  7.9 192.5 %all-gather.9.cloned.1.call-start = ((), (), s32[]{:S(2)}) async-start(), calls=%async_computation.7 | async-start | bytes 1216512 | tf_op jit(solution)/shard_map/all_gather | solution.py:77
  8.7 206.0 %all-gather.11.cloned.1.call-start = ((), (), s32[]{:S(2)}) async-start(), calls=%async_computation.8 | async-start | bytes 4866048 | tf_op jit(solution)/shard_map/all_gather | solution.py:128
  9.4 275.5 %all-gather.13.cloned.1.call-start = ((), (), s32[]{:S(2)}) async-start(), calls=%async_computation.9 | async-start | bytes 4866048 | tf_op jit(solution)/shard_map/all_gather | solution.py:130
  10.0 306.1 %all-gather.15.cloned.1.call-start = ((), (), s32[]{:S(2)}) async-start(), calls=%async_computation.10 | async-start | bytes 1216512 | tf_op jit(solution)/shard_map/all_gather | solution.py:134
  10.6 362.8 %all-gather.17.cloned.1.call-start = ((), (), s32[]{:S(2)}) async-start(), calls=%async_computation.11 | async-start | bytes 1622016 | tf_op jit(solution)/shard_map/all_gather | solution.py:161
  61.5 15.5 %copy-start.18 = (f32[32,32]{1,0:T(8,128)}, f32[32,32]{1,0:T(8,128)S(1)}, u32[]{:S(2)}) copy-start(f32[32,32]{1,0:T(8,128)S(1)} %get-tuple-element.144) | copy-start | bytes 12292
  68.2 216.6 %copy-start.35 = (f32[768]{0:T(1024)}, f32[768]{0:T(1024)S(1)}, u32[]{:S(2)}) copy-start(f32[768]{0:T(1024)S(1)} %convert_element_type.149) | copy-start | bytes 9220
  68.8 9.5 copy-start.6
  166.1 11.4 copy-start.16
  210.6 2.6 copy-start.2
  214.1 0.6 copy-start.21
  214.7 70.2 %copy-start.37 = (f32[768]{0:T(1024)S(1)}, f32[768]{0:T(1024)}, u32[]{:S(2)}) copy-start(f32[768]{0:T(1024)} %convert_element_type.153) | copy-start | bytes 9220
  304.5 2.6 copy-start.1
  304.5 0.9 copy-start.20
  304.5 0.9 copy-start.23
  304.5 0.9 copy-start.29
  305.4 10.6 copy-start.28
  307.1 1.7 copy-start.11
  318.5 160.8 %reduce-scatter.9.cloned.1.call-start = ((), (), s32[]{:S(2)}) async-start(), calls=%async_computation.12 | async-start | bytes 3244032 | tf_op jit(solution)/shard_map/reduce_scatter | solution.py:187
  378.7 5.6 copy-start.9
  378.7 105.3 %copy-start.10 = (bf16[768,768]{1,0:T(8,128)(2,1)S(1)}, bf16[768,768]{1,0:T(8,128)(2,1)}, u32[]{:S(2)}) copy-start(bf16[768,768]{1,0:T(8,128)(2,1)} %all-gather.15.cloned.1.call-done) | copy-start | bytes 3538948
  378.7 473.9 %reduce-scatter.17.cloned.1.call-start = ((), (), s32[]{:S(2)}) async-start(), calls=%async_computation.16 | async-start | bytes 2433024 | tf_op jit(solution)/shard_map/reduce_scatter | solution.py:218
  484.0 368.6 %reduce-scatter.11.cloned.1.call-start = ((), (), s32[]{:S(2)}) async-start(), calls=%async_computation.13 | async-start | bytes 2433024 | tf_op jit(solution)/shard_map/reduce_scatter | solution.py:267
  484.5 18.6 %slice-start = ((s8[6291456]{0:T(1024)(128)(4,1)}), s8[2097152]{0:T(1024)(128)(4,1)S(1)}, s32[]{:S(2)}) async-start(s8[6291456]{0:T(1024)(128)(4,1)} %bitcast.106), calls=%async_computation.18 | async-start | bytes 4194304
  491.5 11.6 copy-start
  491.5 11.7 %slice-start.1 = ((s8[6291456]{0:T(1024)(128)(4,1)}), s8[4194304]{0:T(1024)(128)(4,1)S(1)}, s32[]{:S(2)}) async-start(s8[6291456]{0:T(1024)(128)(4,1)} %bitcast.106), calls=%async_computation.19 | async-start | bytes 8388608
  506.9 6.3 copy-start.5
  513.2 29.3 %copy-start.12 = (bf16[2048,768]{1,0:T(8,128)(2,1)}, bf16[2048,768]{1,0:T(8,128)(2,1)S(1)}, u32[]{:S(2)}) copy-start(bf16[2048,768]{1,0:T(8,128)(2,1)S(1)} %get-tuple-element.120) | copy-start | bytes 9437188
  542.5 19.7 %copy-start.22 = (f32[2048]{0:T(1024)S(1)}, f32[2048]{0:T(1024)}, u32[]{:S(2)}) copy-start(f32[2048]{0:T(1024)} %copy-done.21) | copy-start | bytes 24580
  566.5 6.3 copy-start.4
  566.5 6.3 copy-start.24
  566.5 8.0 copy-start.15
  572.8 1.7 copy-start.13
  584.6 17.4 %copy-start.17 = (f32[64,12,32]{2,1,0:T(8,128)S(1)}, f32[64,12,32]{2,1,0:T(8,128)}, u32[]{:S(2)}) copy-start(f32[64,12,32]{2,1,0:T(8,128)} %copy-done.16) | copy-start | bytes 294916
  612.1 9.7 copy-start.3
  612.1 9.7 copy-start.8
  612.2 9.7 copy-start.14
  646.9 222.3 %reduce-scatter.19.cloned.1.call-start = ((), (), s32[]{:S(2)}) async-start(), calls=%async_computation.17 | async-start | bytes 7299072
  672.6 30.4 %copy-start.7 = (bf16[2,32,32,768]{3,2,1,0:T(8,128)(2,1)S(1)}, bf16[2,32,32,768]{3,2,1,0:T(8,128)(2,1)}, u32[]{:S(2)}) copy-start(bf16[2,32,32,768]{3,2,1,0:T(8,128)(2,1)} %param.21) | copy-start | bytes 9437188
  723.1 288.4 %reduce-scatter.15.cloned.1.call-start = ((), (), s32[]{:S(2)}) async-start(), calls=%async_computation.15 | async-start | bytes 9732096 | tf_op jit(solution)/shard_map/reduce_scatter | solution.py:214
  739.4 0.7 copy-start.36
  739.4 413.0 %reduce-scatter.13.cloned.1.call-start = ((), (), s32[]{:S(2)}) async-start(), calls=%async_computation.14 | async-start | bytes 9732096 | tf_op jit(solution)/shard_map/reduce_scatter | solution.py:212
  758.5 0.7 copy-start.38
  758.5 1.9 copy-start.19
  758.5 33.9 %copy-start.26 = (f32[768]{0:T(1024)S(1)}, f32[768]{0:T(1024)}, u32[]{:S(2)}) copy-start(f32[768]{0:T(1024)} %get-tuple-element.117) | copy-start | bytes 9220
  758.5 33.9 %copy-start.27 = (f32[768]{0:T(1024)S(1)}, f32[768]{0:T(1024)}, u32[]{:S(2)}) copy-start(f32[768]{0:T(1024)} %get-tuple-element.84) | copy-start | bytes 9220
  758.5 33.9 %copy-start.30 = (f32[768]{0:T(1024)S(1)}, f32[768]{0:T(1024)}, u32[]{:S(2)}) copy-start(f32[768]{0:T(1024)} %get-tuple-element.119) | copy-start | bytes 9220
  758.5 33.9 %copy-start.31 = (f32[768]{0:T(1024)S(1)}, f32[768]{0:T(1024)}, u32[]{:S(2)}) copy-start(f32[768]{0:T(1024)} %get-tuple-element.121) | copy-start | bytes 9220
  758.5 33.9 %copy-start.32 = (f32[3072]{0:T(1024)S(1)}, f32[3072]{0:T(1024)}, u32[]{:S(2)}) copy-start(f32[3072]{0:T(1024)} %get-tuple-element.158) | copy-start | bytes 36868
  758.6 33.9 %copy-start.33 = (f32[768]{0:T(1024)S(1)}, f32[768]{0:T(1024)}, u32[]{:S(2)}) copy-start(f32[768]{0:T(1024)} %get-tuple-element.86) | copy-start | bytes 9220
  758.6 33.9 %copy-start.34 = (f32[768]{0:T(1024)S(1)}, f32[768]{0:T(1024)}, u32[]{:S(2)}) copy-start(f32[768]{0:T(1024)} %get-tuple-element.88) | copy-start | bytes 9220
  758.6 80.8 %copy-start.25 = (f32[2048]{0:T(1024)S(1)}, f32[2048]{0:T(1024)}, u32[]{:S(2)}) copy-start(f32[2048]{0:T(1024)} %copy-done.24) | copy-start | bytes 24580
Sparse Core Ops, SparseCore 0:
  10.9 63.0 all-gather.6
  76.9 52.8 all-gather.8
  132.7 62.4 all-gather.10
  198.0 62.3 all-gather.12
  263.1 52.8 all-gather.14
  319.4 53.9 all-gather.16
  378.8 100.4 reduce-scatter.8
  485.2 97.9 reduce-scatter.16
  647.0 97.9 reduce-scatter.10
  751.0 118.0 reduce-scatter.18
  876.7 134.7 reduce-scatter.14
  1017.8 134.5 reduce-scatter.12
